TPU v7x, 512 devices: a whole 4x8x8 slice. The times are simulated.
512 devices in a mesh: tok: 32 (over z_lo, y), store: 16 (over z_hi, x, core).
Axes of the slice: x: 4, y: 8, z: 8 (z_hi: 2, z_lo: 4; z = z_hi * 4 + z_lo), core: 2. Of those that a mesh axis runs over, the one named last changes fastest.
Arguments:
- activations: bfloat16 [32, 1024, 14336], P('store', 'tok'), may hold values from -6 to 6
- out_grads: bfloat16 [32, 1024, 4096], P('store', 'tok'), may hold values from -6 to 6
- validity: int32 [32, 1024], P('store', 'tok'), may hold values 0 or 1
- proj_in: bfloat16 [14336, 64], P('tok'), may hold values from -0.046875 to 0.046875
- proj_out: bfloat16 [4096, 64], P('tok'), may hold values from -0.09375 to 0.09375
- precond: bfloat16 [4096, 4096], P(('tok', 'store')), may hold values from -0.05 to 2.05, as said below
- queries: bfloat16 [1024, 4096], P('store'), may hold values from -0.09375 to 0.09375
- store_rows: float32 [65536, 4096], P(('tok', 'store')), may hold values from -6 to 6
- plan: int32 [16, 512], P(None, ('tok', 'store')), may hold values 0 or 1
Outputs:
- scores: float32 [1024, 65536], P(None, ('tok', 'store'))
- precond_docs: float32 [32, 4096], P('store', 'tok')
- doc_scores: float32 [1024, 32], P('store')
Inputs may be any that keep to these rules, and one draw needn't show every extreme that they name: `precond`: symmetric positive definite. `validity`: 1 marks a real token. `plan`: 1 where the query block is scored against the store block.
All inputs are finite; a program needn't handle non-finite values. No bound on the sum of `validity` on one device may be relied on, other than what follows from the above.
Results may differ from a plain program's by a relative error of at most 0.0049.
Values may be sent and summed in bfloat16 or wider, within the bound.
A program may use at most 64 MiB of HBM per device.

v0:
```python
import math

import jax
import jax.numpy as jnp
from jax import lax
from jax.sharding import PartitionSpec as P


def local(activations, out_grads, validity, proj_in, proj_out, precond, queries, store_rows, plan):
    tok_count = lax.axis_size("tok")
    store_count = lax.axis_size("store")
    doc_local = activations.shape[0]
    len_local = activations.shape[1]
    flat_acts = activations.reshape(doc_local * len_local, activations.shape[2])
    flat_grads = out_grads.reshape(doc_local * len_local, out_grads.shape[2])
    left_acc = jnp.dot(
        flat_acts,
        lax.all_gather(proj_in, "tok", axis=0, tiled=True),
        preferred_element_type=jnp.float32,
    )
    right_acc = jnp.dot(
        flat_grads,
        lax.all_gather(proj_out, "tok", axis=0, tiled=True),
        preferred_element_type=jnp.float32,
    )
    left_proj = left_acc.astype(jnp.bfloat16).reshape(doc_local, len_local, -1)
    right_proj = right_acc.astype(jnp.bfloat16).reshape(doc_local, len_local, -1)
    masked = right_proj.astype(jnp.float32) * validity.astype(jnp.float32)[:, :, None]
    norm_scale = 1.0 / math.sqrt(len_local * tok_count)
    partial_value = (
        jnp.einsum(
            "dpo,dpi->doi", masked, left_proj.astype(jnp.float32), precision=lax.Precision.HIGHEST
        ).reshape(doc_local, -1)
        * norm_scale
    )
    k_total = partial_value.shape[1]
    block_rows = precond.shape[0]
    summed = lax.psum(partial_value, "tok").astype(jnp.bfloat16)
    every_doc = lax.all_gather(summed, "store", axis=0, tiled=True)
    own_block = lax.axis_index("tok") * store_count + lax.axis_index("store")
    grad_block = lax.dynamic_slice_in_dim(every_doc, own_block * block_rows, block_rows, 1)
    partial_pre = jnp.dot(grad_block, precond, preferred_element_type=jnp.float32)
    full_pre = lax.psum(partial_pre, ("tok", "store"))
    cols_tok = k_total // tok_count
    precond_docs = lax.dynamic_slice(
        full_pre,
        (lax.axis_index("store") * doc_local, lax.axis_index("tok") * cols_tok),
        (doc_local, cols_tok),
    )
    doc_scores = lax.dot_general(
        queries.astype(jnp.float32),
        full_pre,
        (((1,), (1,)), ((), ())),
        precision=lax.Precision.HIGHEST,
    )
    query_dev = queries.shape[0]
    row_weights = plan.astype(jnp.float32)[:, 0]
    segment = lax.all_gather(queries, "store", axis=0, tiled=True)
    raw_scores = lax.dot_general(
        segment.astype(jnp.float32),
        store_rows,
        (((1,), (1,)), ((), ())),
        precision=lax.Precision.HIGHEST,
    )
    owners = lax.iota(jnp.int32, segment.shape[0]) // query_dev
    onehot = (owners[:, None] == lax.iota(jnp.int32, store_count)[None, :]).astype(jnp.float32)
    scores = raw_scores * jnp.dot(onehot, row_weights, precision=lax.Precision.HIGHEST)[:, None]
    return (scores, precond_docs, doc_scores)


def solution(mesh):
    return jax.shard_map(
        local,
        mesh=mesh,
        in_specs=(
            P("store", "tok", None),
            P("store", "tok", None),
            P("store", "tok"),
            P("tok", None),
            P("tok", None),
            P(("tok", "store"), None),
            P("store", None),
            P(("tok", "store"), None),
            P(None, ("tok", "store")),
        ),
        out_specs=(P(None, ("tok", "store")), P("store", "tok"), P("store", None)),
        check_vma=False,
    )
```

profile of v0, /device:TPU:1, one launch (start us, length us, event | category | flops | bytes accessed | tf_op | source)
XLA Modules:
  0.0 702.9 jit_solution(10565055672906576047)
XLA Ops:
  8.0 0.0 copy-start
  8.0 0.0 all-gather.7.cloned.1.call-start
  8.1 0.7 all-gather.7.cloned.1.call-update
  8.7 0.0 all-reduce.2.cloned.1.call-start
  8.8 0.7 convert_element_type.29
  9.5 72.2 %all_gather.13 = bf16[4096,64]{0,1:T(8,128)(2,1)S(1)} all-gather(bf16[128,64]{0,1:T(8,128)(2,1)} %param.13), channel_id=1, replica_groups=mesh['tok'=32,'store'=16] {'tok'}, dimensions={0}, use_global_device_ids=true | all-gather | bytes 540672 | tf_op jit(solution)/shard_map/all_gather | solution.py:23
  81.7 1.3 convolution_convert_fusion.1
  83.1 66.3 %all-gather.7.cloned.1.call-done = bf16[32,448,64]{1,2,0:T(8,128)(2,1)} async-done(((bf16[1,448,64]{1,2,0:T(8,128)(2,1)}), bf16[32,448,64]{1,2,0:T(8,128)(2,1)}) %all-gather.7.cloned.1.call-update) | async-done | bytes 1835024 | tf_op jit(solution)/shard_map/all_gather | solution.py:18
  149.4 4.1 copy.13
  153.5 4.7 reshape.41
  158.1 0.0 copy-start.2
  158.1 2.7 convolution_convert_fusion
  160.8 0.0 copy-start.3
  160.9 0.0 copy-start.1
  160.9 0.3 convolution_multiply_fusion.1
  161.2 0.1 mul.43
  161.3 123.8 %psum.14 = bf16[2,4096]{1,0:T(2,128)(2,1)S(1)} all-reduce(f32[2,4096]{1,0:T(2,128)S(1)} %mul.43), channel_id=1, replica_groups=mesh['tok'=32,'store'=16] {'tok'}, use_global_device_ids=true, to_apply=%region_0.0 | all-reduce | flops 8192 | bytes 49152 | tf_op jit(solution)/shard_map/psum | solution.py:38
  285.1 79.7 %all-gather.1 = bf16[16,2,4096]{2,1,0:T(2,128)(2,1)S(1)} all-gather(bf16[1,2,4096]{2,1,0:T(2,128)(2,1)S(1)} %bitcast.30), channel_id=1, replica_groups=mesh['tok'=32,'store'=16] {'store'}, dimensions={0}, use_global_device_ids=true | all-gather | bytes 278528 | tf_op jit(solution)/shard_map/all_gather | solution.py:39
  364.8 0.1 reshape.43
  364.9 0.0 copy-done.2
  364.9 1.1 fusion.3
  366.0 0.0 all-reduce.2.cloned.1.call-update
  366.0 0.0 all-gather.5.cloned.1.call-start
  366.1 0.5 all-gather.5.cloned.1.call-update
  366.6 0.0 copy-done.3
  366.6 0.4 fusion
  367.1 315.1 %all-reduce.2.cloned.1.call-done = f32[32,4096]{1,0:T(8,128)} async-done(((f32[32,4096]{1,0:T(8,128)}), f32[32,4096]{1,0:T(8,128)}) %all-reduce.2.cloned.1.call-update) | async-done | bytes 524304 | tf_op jit(solution)/shard_map/psum | solution.py:43
  682.2 1.3 dynamic_slice.7
  683.5 0.0 copy-done.1
  683.5 2.2 convolution_bitcast_fusion
  685.7 0.0 copy-done
  685.7 9.8 %convolution_multiply_fusion = f32[1024,128]{1,0:T(8,128)} fusion(bf16[1024,4096]{1,0:T(8,128)(2,1)} %all-gather.5.cloned.1.call-done, f32[128,4096]{1,0:T(8,128)S(1)} %copy-done, f32[1024]{0:T(1024)S(1)} %bitcast.27), kind=kOutput, calls=%fused_computation | convolution fusion | flops 6442582016 | bytes 11014144 | tf_op jit(solution)/shard_map/dot_general | solution.py:59
  (2 shorter events, 0.0 us)
Async XLA Ops:
  8.0 677.7 %copy-start = (f32[128,4096]{1,0:T(8,128)S(1)}, f32[128,4096]{1,0:T(8,128)}, u32[]{:S(2)}) copy-start(f32[128,4096]{1,0:T(8,128)} %param.16) | copy-start | bytes 6291460
  8.0 141.4 %all-gather.7.cloned.1.call-start = ((), (), s32[]{:S(2)}) async-start(), calls=%async_computation.2 | async-start | bytes 2162688 | tf_op jit(solution)/shard_map/all_gather | solution.py:18
  8.7 673.4 %all-reduce.2.cloned.1.call-start = ((), (), s32[]{:S(2)}) async-start(), calls=%async_computation.1 | async-start | bytes 1048576 | tf_op jit(solution)/shard_map/psum | solution.py:43
  158.1 206.8 %copy-start.2 = (bf16[8,4096]{1,0:T(8,128)(2,1)S(1)}, bf16[8,4096]{1,0:T(8,128)(2,1)}, u32[]{:S(2)}) copy-start(bf16[8,4096]{1,0:T(8,128)(2,1)} %param.14) | copy-start | bytes 196612
  160.8 205.8 %copy-start.3 = (s32[16,1]{0,1:T(1,128)S(1)}, s32[16,1]{0,1:T(1,128)}, u32[]{:S(2)}) copy-start(s32[16,1]{0,1:T(1,128)} %param.17) | copy-start | bytes 196
  160.9 522.6 %copy-start.1 = (bf16[64,4096]{1,0:T(8,128)(2,1)S(1)}, bf16[64,4096]{1,0:T(8,128)(2,1)}, u32[]{:S(2)}) copy-start(bf16[64,4096]{1,0:T(8,128)(2,1)} %param.15) | copy-start | bytes 1572868
  366.0 319.6 %all-gather.5.cloned.1.call-start = ((), (), s32[]{:S(2)}) async-start(), calls=%async_computation | async-start | bytes 8912896 | tf_op jit(solution)/shard_map/all_gather | solution.py:58
Sparse Core Ops, SparseCore 0:
  10.9 138.4 all-gather.6
  366.1 315.9 all-reduce.1
Sparse Core Ops, SparseCore 1:
  369.8 105.2 all-gather.4
where the time goes:
time: 703 us
  waiting for transfers between devices  383 us (54%)
  blocking collectives  276 us (39%)
  matrix products  17.8 us (3%)
  between operations  15.6 us (2%)
  local copies, waits for them, and re-layouts  10.3 us (1%)
    psum x1, waiting for transfers between devices, local(): full_pre = lax.psum(partial_pre, ('tok', 'store'))  315 us
    psum x1, blocking collectives, local(): summed = lax.psum(partial_value, 'tok').astype(jnp.bfloat16)  124 us
    all_gather x1, blocking collectives, local(): every_doc = lax.all_gather(summed, 'store', axis=0, tiled=True)  79.7 us
    all_gather x1, blocking collectives, local(): lax.all_gather(proj_out, 'tok', axis=0, tiled=True)  72.2 us
    all_gather x1, waiting for transfers between devices, local(): lax.all_gather(proj_in, 'tok', axis=0, tiled=True)  66.3 us
  transfers between devices with their start and end apart: 3, of which 2 were waited for; matrix products, arithmetic and copies ran while one was open for 1% of the time, Pallas kernels for 0%

commit v1 on v0

v1 whole, which is shorter than its diff:
```python
import functools
import math

import jax
import jax.numpy as jnp
from jax import lax
from jax.experimental import pallas as pl
from jax.experimental.pallas import tpu as pltpu
from jax.sharding import PartitionSpec as P

MESH = pl.DeviceIdType.MESH
NT, NS = 32, 16
WIN = 512
PW = 640
QCOLS = 4096
F32 = jnp.float32
BF16 = jnp.bfloat16

UP = [(0, 0), (0, -1), (0, 1), (0, 2)] + [(-k, d) for k in (1, 2) for d in (0, -1, 1, 2)] + [(-3, 0), (-3, -1)]
DN = [(0, 0), (0, 1), (0, -1), (0, 2)] + [(k, d) for k in (1, 2) for d in (0, 1, -1, 2)] + [(3, 1), (3, 2)]
NY = len(UP)
NSPLIT = 2
NZ = 8 * NSPLIT
ZCOLS = QCOLS // NSPLIT
PLAN_Y = 0
PLAN_RS = 7
PLAN_AG = 6


def nt_dot(a, b):
    return lax.dot_general(a, b, (((1,), (1,)), ((), ())), preferred_element_type=F32)


def kernel(
    plan_ref, valid_ref, pt_ref, act_ref, og_ref, prec_ref, q_ref, rows_ref,
    scores_ref, pdoc_ref, dsc_ref,
    ptall, act, og, rows, rowsb, qall, rall, part, rsbuf, gown, gt, gs, ary, arz, arsrc, arsrc2, qp,
    lsem, pz_r, pyu_r, pyd_r, xs_r, zu_r, zd_r, one_r, snd,
):
    t = lax.axis_index("tok")
    s = lax.axis_index("store")
    zl, y = t // 8, t % 8
    zh, x, c = s // 8, (s // 2) % 4, s % 2
    z = zh * 4 + zl

    def at_z(d):
        zz = (z + 8 + d) % 8
        return ((zz % 4) * 8 + y, (zz // 4) * 8 + x * 2 + c)

    def at_y(d):
        return (zl * 8 + (y + 8 + d) % 8, s)

    def at_x(d):
        return (t, zh * 8 + ((x + 4 + d) % 4) * 2 + c)

    partner = (t, zh * 8 + x * 2 + (1 - c))
    other = (1 - zh) * 8 + x * 2 + c

    def rcopy(src, dst, ss, rs, dev):
        return pltpu.make_async_remote_copy(
            src_ref=src, dst_ref=dst, send_sem=ss, recv_sem=rs, device_id=dev, device_id_type=MESH
        )

    def drain(ref, sem):
        rcopy(ref, ref, snd.at[0], sem, partner).wait_recv()

    def sent(ref, sem):
        rcopy(ref, ref, sem, one_r.at[0], partner).wait_send()

    def qsrc(k, j):
        return q_ref.at[k, :, pl.ds(j * ZCOLS, ZCOLS)]

    R_PSH, R_QSH, R_RZ, R_RX, R_RX2, R_RSH, R_RS, R_GT, R_GS, R_ARY, R_ARZ = range(11)
    (S_PZ, S_PZH, S_PY, S_PSH, S_X, S_Z, S_QSH, S_RZ, S_RX, S_RX2, S_RSH, S_RS, S_GT, S_GS, S_ARY, S_ARZ) = range(16)

    loc = []

    def lcopy(src, dst):
        cp = pltpu.make_async_copy(src, dst, lsem.at[len(loc)])
        cp.start()
        loc.append(cp)
        return cp

    l_pt = lcopy(pt_ref, ptall.at[t])
    l_pr = lcopy(prec_ref, rall.at[s])
    for k in range(4):
        for j in range(NSPLIT):
            pltpu.make_async_copy(qsrc(k, j), qall.at[s, k, j], xs_r.at[0, k, j]).start()
    l_a = [lcopy(act_ref.at[d], act.at[pl.ds(32 * d, 32)]) for d in range(2)]
    l_o = [lcopy(og_ref.at[d], og.at[pl.ds(32 * d, 32)]) for d in range(2)]
    l_r = lcopy(rows_ref, rows)

    barrier = pltpu.get_barrier_semaphore()

    def greet(dev):
        pl.semaphore_signal(barrier, inc=1, device_id=dev, device_id_type=MESH)

    greet(at_z(1))
    greet(at_z(-1))

    @pl.loop(1, NT)
    def _(k):
        greet(((t + k) % NT, s))

    @pl.loop(1, NS)
    def _(k):
        greet((t, (s + k) % NS))

    pl.semaphore_wait(barrier, NT - 1 + NS - 1 + 2)

    half = pl.ds(2 * c, 2)

    def slot(dy, dz):
        return ((zl + 4 + dz) % 4) * 8 + (y + 8 + dy) % 8

    def psend(sl, rowsl, ss, rs, dev):
        ref = ptall.at[sl, rowsl]
        rcopy(ref, ref, ss, rs, dev).start()

    def pshare(sl):
        psend(sl, half, snd.at[S_PSH], one_r.at[R_PSH], partner)

    l_pt.wait()
    psend(t, half, snd.at[S_PZ], pz_r.at[0], at_z(1))
    psend(t, half, snd.at[S_PZ], pz_r.at[1], at_z(-1))

    def pwait(sem, n=2):
        drain(ptall.at[0, pl.ds(0, n)], sem)

    for k in range(4):
        for j in range(NSPLIT):
            dst = qall.at[s, k, j]
            rcopy(qsrc(k, j), dst, snd.at[S_X], xs_r.at[2, k, j], at_x(1)).start()
            rcopy(qsrc(k, j), dst, snd.at[S_X], xs_r.at[1, k, j], at_x(-1)).start()

    rcopy(prec_ref, rall.at[s], snd.at[S_RZ], one_r.at[R_RZ], (t, other)).start()
    for d in (1, -1, 2):
        rcopy(prec_ref, rall.at[s], snd.at[S_RX], one_r.at[R_RX], at_x(d)).start()

    def need(order, k, d):
        dy, dz = order[k]
        return 0 if dy == 0 else order.index((dy + d, dz)) + 1

    got = [0, 0]

    def yrecv_to(side, n):
        order, sems, d = ((UP, pyu_r, -1), (DN, pyd_r, 1))[side]
        while got[side] < n:
            k = got[side]
            pwait(sems.at[k])
            pshare(slot(order[k][0] + d, order[k][1]))
            got[side] += 1

    def ysend(k):
        yrecv_to(0, need(UP, k, 1))
        psend(slot(*UP[k]), half, snd.at[S_PY], pyu_r.at[k], at_y(1))
        yrecv_to(1, need(DN, k, -1))
        psend(slot(*DN[k]), half, snd.at[S_PY], pyd_r.at[k], at_y(-1))

    def xorder(i):
        return i + i // 2 - 2 * (i // 3)

    def zchunk(n, group, up):
        xi, k, j = n // (2 * NSPLIT), (n // NSPLIT) % 2, n % NSPLIT
        sl = group * 8 + ((x + xorder(xi)) % 4) * 2 + c
        return qall.at[sl, k + (0 if up else 2), j]

    def qwait(i, k, j):
        if i == 0:
            pltpu.make_async_copy(qsrc(k, j), qall.at[s, k, j], xs_r.at[0, k, j]).wait()
        else:
            drain(qall.at[0, 0, 0], xs_r.at[i, k, j])

    def qshare(ref):
        rcopy(ref, ref, snd.at[S_QSH], one_r.at[R_QSH], partner).start()

    def own_group(xi, k, j):
        return qall.at[zh * 8 + ((x + [0, 1, 3, 2][xi]) % 4) * 2 + c, k, j]

    def zstep(tau):
        if tau < NZ:
            xi, k, j = tau // (2 * NSPLIT), (tau // NSPLIT) % 2, tau % NSPLIT
            for i in {0: (0,), 1: (1, 2), 2: (), 3: (3,)}[xi]:
                for kk in (k, k + 2):
                    qwait(i, kk, j)
                    qshare(own_group(i, kk, j))
            if xi == 1:
                lref = own_group(2, k, j)
                rcopy(lref, lref, snd.at[S_X], xs_r.at[3, k, j], at_x(1)).start()
                rref = own_group(1, k + 2, j)
                rcopy(rref, rref, snd.at[S_X], xs_r.at[3, k + 2, j], at_x(-1)).start()
        if tau < NZ:

            @pl.when(zl == 3)
            def _():
                ref = zchunk(tau, zh, True)
                rcopy(ref, ref, snd.at[S_Z], zu_r.at[tau], at_z(1)).start()

            @pl.when(zl == 0)
            def _():
                ref = zchunk(tau, zh, False)
                rcopy(ref, ref, snd.at[S_Z], zd_r.at[tau], at_z(-1)).start()

        u = tau - zl

        @pl.when((u >= 0) & (u < NZ))
        def _():
            ref = zchunk(u, 1 - zh, True)
            drain(ref, zu_r.at[u])

            @pl.when(zl != 3)
            def _():
                rcopy(ref, ref, snd.at[S_Z], zu_r.at[u], at_z(1)).start()

            qshare(ref)

        v = tau - 3 + zl

        @pl.when((v >= 0) & (v < NZ))
        def _():
            ref = zchunk(v, 1 - zh, False)
            drain(ref, zd_r.at[v])

            @pl.when(zl != 0)
            def _():
                rcopy(ref, ref, snd.at[S_Z], zd_r.at[v], at_z(-1)).start()

            qshare(ref)

    nsteps = NZ + 3
    zs = iter(range(nsteps))

    def zrun(n):
        for _ in range(n):
            tau = next(zs, None)
            if tau is None:
                return
            zstep(tau)

    ysend(0)
    pwait(pz_r.at[0])
    psend(slot(0, -1), pl.ds(2 * c, 1), snd.at[S_PZH], pz_r.at[2], at_z(1))
    pwait(pz_r.at[1])
    psend(slot(0, 1), pl.ds(2 * c + 1, 1), snd.at[S_PZH], pz_r.at[3], at_z(-1))
    ysend(1)
    ysend(2)
    pshare(slot(0, -1))
    pshare(slot(0, 1))
    pwait(pz_r.at[2], 1)
    pwait(pz_r.at[3], 1)
    ysend(3)
    pshare(slot(0, 2))
    for k in range(4, NY):
        ysend(k)
        if k % 4 == 0:
            zrun(PLAN_Y)
    drain(rall.at[0], one_r.at[R_RZ])
    for d in (1, -1, 2):
        rcopy(rall.at[other], rall.at[other], snd.at[S_RX2], one_r.at[R_RX2], at_x(d)).start()
    yrecv_to(0, NY)
    yrecv_to(1, NY)
    drain(rall.at[pl.ds(0, 3)], one_r.at[R_RX])

    l_r.wait()
    rowsb[...] = rows[...].astype(BF16)
    for cp in l_a + l_o:
        cp.wait()
    drain(ptall.at[pl.ds(0, NT - 1), pl.ds(0, 2)], one_r.at[R_PSH])

    def project(i, acc):
        left, right = acc
        start = pl.multiple_of(448 * i - 64 * (i % 2), 128)
        w = ptall[i].reshape(64, PW)
        left = left + nt_dot(act[:, pl.ds(start, WIN)], w[:, :WIN])
        right = right + nt_dot(w[:, WIN:], og[:, pl.ds(pl.multiple_of(128 * i, 128), 128)])
        return left, right

    zero = jnp.zeros((64, 64), F32)
    left, right = lax.fori_loop(0, NT, project, (zero, zero))
    left = left.astype(BF16)
    right = right.astype(BF16)
    r0 = lax.broadcasted_iota(jnp.int32, (64, 64), 0)
    r1 = lax.broadcasted_iota(jnp.int32, (64, 64), 1)
    pick = (r1 == 2 * (r0 % 32) + r0 // 32).astype(F32).astype(BF16)
    right = jnp.dot(pick, right, preferred_element_type=F32)
    for d in range(2):
        masked = (right * valid_ref[pl.ds(d, 1), :]).astype(BF16)
        outer = jnp.dot(masked, left, preferred_element_type=F32)
        part[:, d, :] = jnp.concatenate([outer[:32], outer[32:]], axis=1)

    @pl.loop(1, NT)
    def _(k):
        to = (t + k) % NT
        rcopy(part.at[to], rsbuf.at[t], snd.at[S_RS], one_r.at[R_RS], (to, s)).start()

    rsbuf[t] = part[t]
    zrun(PLAN_RS)
    drain(rsbuf.at[pl.ds(0, NT - 1)], one_r.at[R_RS])
    total = jnp.sum(rsbuf[...], axis=0) * (1.0 / 32.0)
    gown[...] = total.astype(BF16).astype(F32)
    gt[t] = gown[...]
    gs[s] = gown[...]

    @pl.loop(1, NS)
    def _(k):
        rcopy(gown, gs.at[s], snd.at[S_GS], one_r.at[R_GS], (t, (s + k) % NS)).start()

    @pl.loop(1, NT)
    def _(k):
        rcopy(gown, gt.at[t], snd.at[S_GT], one_r.at[R_GT], ((t + k) % NT, s)).start()

    l_pr.wait()
    drain(rall.at[pl.ds(0, 3)], one_r.at[R_RX2])

    @pl.loop(0, 8)
    def _(k):
        ref = rall.at[2 * k + c]
        rcopy(ref, ref, snd.at[S_RSH], one_r.at[R_RSH], partner).start()

    zrun(PLAN_AG)
    drain(rall.at[pl.ds(0, 8)], one_r.at[R_RSH])
    prows = rall[...].astype(F32).reshape(128, 4096).astype(BF16)
    for k in range(4):
        own_q = jnp.concatenate([qall[s, k, j] for j in range(NSPLIT)], axis=1)
        qp[pl.ds(16 * k, 16), :] = nt_dot(own_q, prows).astype(BF16)

    drain(gs.at[pl.ds(0, NS - 1)], one_r.at[R_GS])
    docs = jnp.concatenate([gs[:, 0, :], gs[:, 1, :]], axis=0)
    acc = jnp.zeros((16, 128), F32)
    d0 = lax.broadcasted_iota(jnp.int32, (128, 32), 0)
    d1 = lax.broadcasted_iota(jnp.int32, (128, 32), 1)
    for j in range(4):
        put = (d0 == 32 * j + 2 * (d1 % 16) + d1 // 16).astype(F32).astype(BF16)
        spread = jnp.dot(put, docs.astype(BF16), preferred_element_type=F32).astype(BF16)
        acc = acc + nt_dot(qp[pl.ds(16 * j, 16), :], spread)
    arsrc[...] = acc
    ary[y] = acc

    @pl.loop(1, 8)
    def _(k):
        rcopy(arsrc, ary.at[y], snd.at[S_ARY], one_r.at[R_ARY], at_y(k)).start()

    drain(gt.at[pl.ds(0, NT - 1)], one_r.at[R_GT])
    pdoc_ref[...] = nt_dot(jnp.concatenate([gt[i] for i in range(NT)], axis=1).astype(BF16), prows)

    drain(ary.at[pl.ds(0, 7)], one_r.at[R_ARY])
    acc = jnp.sum(ary[...], axis=0)
    arsrc2[...] = acc
    arz[zl] = acc

    @pl.loop(1, 4)
    def _(k):
        rcopy(arsrc2, arz.at[zl], snd.at[S_ARZ], one_r.at[R_ARZ], (((zl + k) % 4) * 8 + y, s)).start()

    zrun(nsteps)
    drain(qall.at[pl.ds(0, 8)], one_r.at[R_QSH])

    @pl.loop(0, NS // 2)
    def _(k):
        raw = jnp.zeros((128, 128), F32)
        for j in range(NSPLIT):
            blk = jnp.concatenate([qall[2 * k + h, i, j] for h in range(2) for i in range(4)], axis=0)
            raw = raw + nt_dot(blk, rowsb[:, ZCOLS * j : ZCOLS * (j + 1)])
        for h in range(2):
            w = plan_ref[2 * k + h].astype(F32)
            scores_ref[pl.ds(pl.multiple_of(128 * k + 64 * h, 64), 64), :] = raw[64 * h : 64 * h + 64] * w

    drain(arz.at[pl.ds(0, 3)], one_r.at[R_ARZ])
    acc = jnp.sum(arz[...], axis=0)
    for j in range(4):
        dsc_ref[pl.ds(16 * j, 16), :] = acc[:, 32 * j : 32 * j + 32]

    sent(ptall.at[pl.ds(0, 2), pl.ds(0, 2)], snd.at[S_PZ])
    sent(ptall.at[0, pl.ds(0, 2)], snd.at[S_PZH])
    sent(ptall.at[pl.ds(0, 2 * NY), pl.ds(0, 2)], snd.at[S_PY])
    sent(ptall.at[pl.ds(0, NT - 1), pl.ds(0, 2)], snd.at[S_PSH])
    sent(qall.at[pl.ds(0, 3)], snd.at[S_X])
    sent(qall.at[pl.ds(0, 4)], snd.at[S_Z])
    sent(qall.at[pl.ds(0, 8)], snd.at[S_QSH])
    sent(rall.at[0], snd.at[S_RZ])
    sent(rall.at[pl.ds(0, 3)], snd.at[S_RX])
    sent(rall.at[pl.ds(0, 3)], snd.at[S_RX2])
    sent(rall.at[pl.ds(0, 8)], snd.at[S_RSH])
    sent(rsbuf.at[pl.ds(0, NT - 1)], snd.at[S_RS])
    sent(gt.at[pl.ds(0, NT - 1)], snd.at[S_GT])
    sent(gs.at[pl.ds(0, NS - 1)], snd.at[S_GS])
    sent(ary.at[pl.ds(0, 7)], snd.at[S_ARY])
    sent(arz.at[pl.ds(0, 3)], snd.at[S_ARZ])


def local(activations, out_grads, validity, proj_in, proj_out, precond, queries, store_rows, plan):
    t = lax.axis_index("tok")
    pin = proj_in.T
    win = jnp.where(t % 2 == 0, jnp.pad(pin, ((0, 0), (0, 64))), jnp.pad(pin, ((0, 0), (64, 0))))
    pt = jnp.concatenate([win, proj_out.T], axis=1).reshape(4, 16, PW)
    own = jnp.eye(2, dtype=F32)[:, :, None] * validity.astype(F32)[None]
    valid = own.reshape(2, 64)
    hbm = pl.BlockSpec(memory_space=pl.ANY)
    vm = pl.BlockSpec(memory_space=pltpu.VMEM)
    sm = pl.BlockSpec(memory_space=pltpu.SMEM)
    dma = pltpu.SemaphoreType.DMA
    return pl.pallas_call(
        kernel,
        out_shape=(
            jax.ShapeDtypeStruct((1024, 128), F32),
            jax.ShapeDtypeStruct((2, 128), F32),
            jax.ShapeDtypeStruct((64, 32), F32),
        ),
        in_specs=[sm, vm, hbm, hbm, hbm, hbm, hbm, hbm],
        out_specs=(vm, vm, vm),
        scratch_shapes=[
            pltpu.VMEM((NT, 4, 16, PW), BF16),
            pltpu.VMEM((64, 14336), BF16),
            pltpu.VMEM((64, 4096), BF16),
            pltpu.VMEM((128, 4096), F32),
            pltpu.VMEM((128, 4096), BF16),
            pltpu.VMEM((NS, 4, NSPLIT, 16, ZCOLS), BF16),
            pltpu.VMEM((NS, 8, 4096), BF16),
            pltpu.VMEM((NT, 2, 128), F32),
            pltpu.VMEM((NT, 2, 128), F32),
            pltpu.VMEM((2, 128), F32),
            pltpu.VMEM((NT, 2, 128), F32),
            pltpu.VMEM((NS, 2, 128), F32),
            pltpu.VMEM((8, 16, 128), F32),
            pltpu.VMEM((4, 16, 128), F32),
            pltpu.VMEM((16, 128), F32),
            pltpu.VMEM((16, 128), F32),
            pltpu.VMEM((64, 128), BF16),
            dma((7,)),
            dma((4,)),
            dma((NY,)),
            dma((NY,)),
            dma((4, 4, NSPLIT)),
            dma((NZ,)),
            dma((NZ,)),
            dma((11,)),
            dma((16,)),
        ],
        compiler_params=pltpu.CompilerParams(collective_id=0, has_side_effects=True),
        name="logra",
    )(
        plan.reshape(16),
        valid,
        pt,
        activations,
        out_grads,
        precond,
        queries.reshape(4, 16, 4096),
        store_rows,
    )


def solution(mesh):
    return jax.shard_map(
        local,
        mesh=mesh,
        in_specs=(
            P("store", "tok", None),
            P("store", "tok", None),
            P("store", "tok"),
            P("tok", None),
            P("tok", None),
            P(("tok", "store"), None),
            P("store", None),
            P(("tok", "store"), None),
            P(None, ("tok", "store")),
        ),
        out_specs=(P(None, ("tok", "store")), P("store", "tok"), P("store", None)),
        check_vma=False,
    )
```

time: 703 us -> 145 us (0.21)
  waiting for transfers between devices: 383 us -> 0 us
  blocking collectives: 276 us -> 0 us
  Pallas kernels: 0 us -> 135 us
  matrix products: 17.8 us -> 0 us
  between operations: 15.6 us -> 0.66 us
    psum x1 -> x0, waiting for transfers between devices: 315 us -> none  [local(): full_pre = lax.psum(partial_pre, ('tok', 'store'))]
    all_gather x2 -> x0, blocking collectives: 152 us -> none  [the longest x1 79.7 us: local(): every_doc = lax.all_gather(summed, 'store', axis=0, tiled=True)]
    pallas_call x0 -> x1, Pallas kernels: none -> 135 us  [local(): pl.pallas_call(kernel, out_shape=(jax.ShapeDtypeStruct((1024, 128), F32),...]
    psum x1 -> x0, blocking collectives: 124 us -> none  [local(): summed = lax.psum(partial_value, 'tok').astype(jnp.bfloat16)]
    all_gather x2 -> x0, waiting for transfers between devices: 66.3 us -> none  [the longest x1 66.3 us: local(): lax.all_gather(proj_in, 'tok', axis=0, tiled=True)]
    dot_general x7 -> x0, matrix products: 17.8 us -> none  [the longest x1 9.77 us: local(): lax.dot_general(segment.astype(jnp.float32), store_rows, (((1,), (1,)), (...]
  transfers between devices with their start and end apart: 3 -> 0, of which waited for: 2 -> 0; matrix products, arithmetic and copies ran while one was open for 1% -> 0% of each run, Pallas kernels for 0% -> 0%
where the time goes in v1:
time: 145 us; the launch traced here: 144 us
  Pallas kernels  135 us (93%)
  local copies, waits for them, and re-layouts  4.74 us (3%)
  other arithmetic  3.62 us (2%)
    pallas_call x1, Pallas kernels, local(): pl.pallas_call(kernel, out_shape=(jax.ShapeDtypeStruct((1024, 128), F32),...  135 us
    unnamed x2, local copies, waits for them, and re-layouts  3.06 us

profile of v1, /device:TPU:1, one launch (start us, length us, event | category | flops | bytes accessed | tf_op | source)
XLA Modules:
  0.0 144.4 jit_solution(14158887478302812345)
XLA Ops:
  0.6 0.7 convert_element_type.15
  1.3 0.1 mul.20
  1.4 0.1 mul.18
  1.5 0.1 mul.19
  1.6 0.6 broadcast_multiply_fusion.valid_ref
  2.1 1.0 pad_select_fusion
  3.1 1.4 pad_maximum_fusion
  4.5 135.4 %logra.1 = (f32[1024,128]{1,0:T(8,128)}, f32[2,128]{1,0:T(2,128)}, f32[64,32]{1,0:T(8,128)}) custom-call(s32[16]{0:T(128)} %bitcast.9, f32[2,64]{1,0:T(2,128)} %broadcast_multiply_fusion.valid_ref, bf16[4,16,640]{2,1,0:T(8,128)(2,1)} %bitcast.6, bf16[2,32,14336]{2,1,0:T(8,128)(2,1)} %act_ref.1, bf16[2,32,4096]{2,1,0:T(8,128)(2,1)} %og_ref.1, ...), custom_call_target="tpu_custom_call" | custom-call | tf_op jit(solution)/shard_map/logra/pallas_call | solution.py:402
  139.9 1.4 copy.12
  141.3 1.9 %copy.15 = f32[1024,128]{1,0:T(8,128)} copy(f32[1024,128]{1,0:T(8,128)} %get-tuple-element.9) | data formatting | bytes 1048576
  143.2 1.2 copy.16
  (1 shorter events, 0.0 us)

commit v2 on v1

--- a/solution.py
+++ b/solution.py
@@ -22,9 +22,10 @@
 NSPLIT = 2
 NZ = 8 * NSPLIT
 ZCOLS = QCOLS // NSPLIT
-PLAN_Y = 0
-PLAN_RS = 7
-PLAN_AG = 6
+LAG = 2
+PLAN_Y = 1
+PLAN_RS = 6
+PLAN_AG = 4
 
 
 def nt_dot(a, b):
@@ -32,7 +33,7 @@
 
 
 def kernel(
-    plan_ref, valid_ref, pt_ref, act_ref, og_ref, prec_ref, q_ref, rows_ref,
+    plan_ref, valid_ref, pin_ref, pout_ref, act_ref, og_ref, prec_ref, q_ref, rows_ref,
     scores_ref, pdoc_ref, dsc_ref,
     ptall, act, og, rows, rowsb, qall, rall, part, rsbuf, gown, gt, gs, ary, arz, arsrc, arsrc2, qp,
     lsem, pz_r, pyu_r, pyd_r, xs_r, zu_r, zd_r, one_r, snd,
@@ -70,7 +71,7 @@
     def qsrc(k, j):
         return q_ref.at[k, :, pl.ds(j * ZCOLS, ZCOLS)]
 
-    R_PSH, R_QSH, R_RZ, R_RX, R_RX2, R_RSH, R_RS, R_GT, R_GS, R_ARY, R_ARZ = range(11)
+    R_PSH, R_PSH2, R_QSA, R_QSB, R_RZ, R_RX, R_RX2, R_RSH, R_RS, R_GT, R_GS, R_ARY, R_ARZ = range(13)
     (S_PZ, S_PZH, S_PY, S_PSH, S_X, S_Z, S_QSH, S_RZ, S_RX, S_RX2, S_RSH, S_RS, S_GT, S_GS, S_ARY, S_ARZ) = range(16)
 
     loc = []
@@ -81,7 +82,6 @@
         loc.append(cp)
         return cp
 
-    l_pt = lcopy(pt_ref, ptall.at[t])
     l_pr = lcopy(prec_ref, rall.at[s])
     for k in range(4):
         for j in range(NSPLIT):
@@ -106,6 +106,18 @@
     def _(k):
         greet((t, (s + k) % NS))
 
+    win = pin_ref[...]
+    gap = jnp.zeros((64, WIN - 448), BF16)
+
+    @pl.when(t % 2 == 0)
+    def _():
+        ptall[t, :, :, :WIN] = jnp.concatenate([win, gap], axis=1).reshape(4, 16, WIN)
+
+    @pl.when(t % 2 == 1)
+    def _():
+        ptall[t, :, :, :WIN] = jnp.concatenate([gap, win], axis=1).reshape(4, 16, WIN)
+
+    ptall[t, :, :, WIN:] = pout_ref[...].reshape(4, 16, PW - WIN)
     pl.semaphore_wait(barrier, NT - 1 + NS - 1 + 2)
 
     half = pl.ds(2 * c, 2)
@@ -117,17 +129,16 @@
         ref = ptall.at[sl, rowsl]
         rcopy(ref, ref, ss, rs, dev).start()
 
-    def pshare(sl):
-        psend(sl, half, snd.at[S_PSH], one_r.at[R_PSH], partner)
-
-    l_pt.wait()
+    def pshare(sl, group=None):
+        psend(sl, half, snd.at[S_PSH], one_r.at[R_PSH if group is None else group], partner)
+
     psend(t, half, snd.at[S_PZ], pz_r.at[0], at_z(1))
     psend(t, half, snd.at[S_PZ], pz_r.at[1], at_z(-1))
 
     def pwait(sem, n=2):
         drain(ptall.at[0, pl.ds(0, n)], sem)
 
-    for k in range(4):
+    for k in (0, 2, 1, 3):
         for j in range(NSPLIT):
             dst = qall.at[s, k, j]
             rcopy(qsrc(k, j), dst, snd.at[S_X], xs_r.at[2, k, j], at_x(1)).start()
@@ -148,7 +159,7 @@
         while got[side] < n:
             k = got[side]
             pwait(sems.at[k])
-            pshare(slot(order[k][0] + d, order[k][1]))
+            pshare(slot(order[k][0] + d, order[k][1]), R_PSH if k < 8 else R_PSH2)
             got[side] += 1
 
     def ysend(k):
@@ -171,8 +182,8 @@
         else:
             drain(qall.at[0, 0, 0], xs_r.at[i, k, j])
 
-    def qshare(ref):
-        rcopy(ref, ref, snd.at[S_QSH], one_r.at[R_QSH], partner).start()
+    def qshare(ref, group):
+        rcopy(ref, ref, snd.at[S_QSH], one_r.at[group], partner).start()
 
     def own_group(xi, k, j):
         return qall.at[zh * 8 + ((x + [0, 1, 3, 2][xi]) % 4) * 2 + c, k, j]
@@ -183,7 +194,7 @@
             for i in {0: (0,), 1: (1, 2), 2: (), 3: (3,)}[xi]:
                 for kk in (k, k + 2):
                     qwait(i, kk, j)
-                    qshare(own_group(i, kk, j))
+                    qshare(own_group(i, kk, j), R_QSA)
             if xi == 1:
                 lref = own_group(2, k, j)
                 rcopy(lref, lref, snd.at[S_X], xs_r.at[3, k, j], at_x(1)).start()
@@ -201,7 +212,7 @@
                 ref = zchunk(tau, zh, False)
                 rcopy(ref, ref, snd.at[S_Z], zd_r.at[tau], at_z(-1)).start()
 
-        u = tau - zl
+        u = tau - LAG * (zl + 1)
 
         @pl.when((u >= 0) & (u < NZ))
         def _():
@@ -212,9 +223,9 @@
             def _():
                 rcopy(ref, ref, snd.at[S_Z], zu_r.at[u], at_z(1)).start()
 
-            qshare(ref)
-
-        v = tau - 3 + zl
+            qshare(ref, R_QSB)
+
+        v = tau - LAG * (4 - zl)
 
         @pl.when((v >= 0) & (v < NZ))
         def _():
@@ -225,9 +236,9 @@
             def _():
                 rcopy(ref, ref, snd.at[S_Z], zd_r.at[v], at_z(-1)).start()
 
-            qshare(ref)
-
-    nsteps = NZ + 3
+            qshare(ref, R_QSB)
+
+    nsteps = NZ + 4 * LAG
     zs = iter(range(nsteps))
 
     def zrun(n):
@@ -236,6 +247,18 @@
             if tau is None:
                 return
             zstep(tau)
+
+    def score(group):
+        @pl.loop(0, 4)
+        def _(k):
+            sl = group * 8 + 2 * k
+            raw = jnp.zeros((128, 128), F32)
+            for j in range(NSPLIT):
+                blk = jnp.concatenate([qall[sl + h, i, j] for h in range(2) for i in range(4)], axis=0)
+                raw = raw + nt_dot(blk, rowsb[:, ZCOLS * j : ZCOLS * (j + 1)])
+            for h in range(2):
+                w = plan_ref[sl + h].astype(F32)
+                scores_ref[pl.ds(pl.multiple_of(64 * (sl + h), 64), 64), :] = raw[64 * h : 64 * h + 64] * w
 
     ysend(0)
     pwait(pz_r.at[0])
@@ -252,31 +275,33 @@
     pshare(slot(0, 2))
     for k in range(4, NY):
         ysend(k)
-        if k % 4 == 0:
-            zrun(PLAN_Y)
+        zrun(PLAN_Y)
     drain(rall.at[0], one_r.at[R_RZ])
     for d in (1, -1, 2):
         rcopy(rall.at[other], rall.at[other], snd.at[S_RX2], one_r.at[R_RX2], at_x(d)).start()
-    yrecv_to(0, NY)
-    yrecv_to(1, NY)
-    drain(rall.at[pl.ds(0, 3)], one_r.at[R_RX])
-
     l_r.wait()
     rowsb[...] = rows[...].astype(BF16)
     for cp in l_a + l_o:
         cp.wait()
-    drain(ptall.at[pl.ds(0, NT - 1), pl.ds(0, 2)], one_r.at[R_PSH])
-
-    def project(i, acc):
+
+    def project(acc, dys):
         left, right = acc
-        start = pl.multiple_of(448 * i - 64 * (i % 2), 128)
-        w = ptall[i].reshape(64, PW)
-        left = left + nt_dot(act[:, pl.ds(start, WIN)], w[:, :WIN])
-        right = right + nt_dot(w[:, WIN:], og[:, pl.ds(pl.multiple_of(128 * i, 128), 128)])
+        for dy in dys:
+            for dz in (0, 1, 2, 3):
+                i = slot(dy, dz)
+                start = pl.multiple_of(448 * i - 64 * (i % 2), 128)
+                w = ptall[i].reshape(64, PW)
+                left = left + nt_dot(act[:, pl.ds(start, WIN)], w[:, :WIN])
+                right = right + nt_dot(w[:, WIN:], og[:, pl.ds(pl.multiple_of(128 * i, 128), 128)])
         return left, right
 
-    zero = jnp.zeros((64, 64), F32)
-    left, right = lax.fori_loop(0, NT, project, (zero, zero))
+    drain(ptall.at[pl.ds(0, 19), pl.ds(0, 2)], one_r.at[R_PSH])
+    acc = project((jnp.zeros((64, 64), F32), jnp.zeros((64, 64), F32)), (0, -1, 1, -2, 2))
+    yrecv_to(0, NY)
+    yrecv_to(1, NY)
+    drain(rall.at[pl.ds(0, 3)], one_r.at[R_RX])
+    drain(ptall.at[pl.ds(0, 12), pl.ds(0, 2)], one_r.at[R_PSH2])
+    left, right = project(acc, (-3, 3, 4))
     left = left.astype(BF16)
     right = right.astype(BF16)
     r0 = lax.broadcasted_iota(jnp.int32, (64, 64), 0)
@@ -284,7 +309,9 @@
     pick = (r1 == 2 * (r0 % 32) + r0 // 32).astype(F32).astype(BF16)
     right = jnp.dot(pick, right, preferred_element_type=F32)
     for d in range(2):
-        masked = (right * valid_ref[pl.ds(d, 1), :]).astype(BF16)
+        live = valid_ref[pl.ds(d, 1), :].astype(F32)
+        rest = jnp.zeros((1, 32), F32)
+        masked = (right * jnp.concatenate([live, rest] if d == 0 else [rest, live], axis=1)).astype(BF16)
         outer = jnp.dot(masked, left, preferred_element_type=F32)
         part[:, d, :] = jnp.concatenate([outer[:32], outer[32:]], axis=1)
 
@@ -295,6 +322,8 @@
 
     rsbuf[t] = part[t]
     zrun(PLAN_RS)
+    drain(qall.at[pl.ds(0, 4)], one_r.at[R_QSA])
+    score(zh)
     drain(rsbuf.at[pl.ds(0, NT - 1)], one_r.at[R_RS])
     total = jnp.sum(rsbuf[...], axis=0) * (1.0 / 32.0)
     gown[...] = total.astype(BF16).astype(F32)
@@ -353,17 +382,8 @@
         rcopy(arsrc2, arz.at[zl], snd.at[S_ARZ], one_r.at[R_ARZ], (((zl + k) % 4) * 8 + y, s)).start()
 
     zrun(nsteps)
-    drain(qall.at[pl.ds(0, 8)], one_r.at[R_QSH])
-
-    @pl.loop(0, NS // 2)
-    def _(k):
-        raw = jnp.zeros((128, 128), F32)
-        for j in range(NSPLIT):
-            blk = jnp.concatenate([qall[2 * k + h, i, j] for h in range(2) for i in range(4)], axis=0)
-            raw = raw + nt_dot(blk, rowsb[:, ZCOLS * j : ZCOLS * (j + 1)])
-        for h in range(2):
-            w = plan_ref[2 * k + h].astype(F32)
-            scores_ref[pl.ds(pl.multiple_of(128 * k + 64 * h, 64), 64), :] = raw[64 * h : 64 * h + 64] * w
+    drain(qall.at[pl.ds(0, 4)], one_r.at[R_QSB])
+    score(1 - zh)
 
     drain(arz.at[pl.ds(0, 3)], one_r.at[R_ARZ])
     acc = jnp.sum(arz[...], axis=0)
@@ -389,12 +409,6 @@
 
 
 def local(activations, out_grads, validity, proj_in, proj_out, precond, queries, store_rows, plan):
-    t = lax.axis_index("tok")
-    pin = proj_in.T
-    win = jnp.where(t % 2 == 0, jnp.pad(pin, ((0, 0), (0, 64))), jnp.pad(pin, ((0, 0), (64, 0))))
-    pt = jnp.concatenate([win, proj_out.T], axis=1).reshape(4, 16, PW)
-    own = jnp.eye(2, dtype=F32)[:, :, None] * validity.astype(F32)[None]
-    valid = own.reshape(2, 64)
     hbm = pl.BlockSpec(memory_space=pl.ANY)
     vm = pl.BlockSpec(memory_space=pltpu.VMEM)
     sm = pl.BlockSpec(memory_space=pltpu.SMEM)
@@ -406,7 +420,7 @@
             jax.ShapeDtypeStruct((2, 128), F32),
             jax.ShapeDtypeStruct((64, 32), F32),
         ),
-        in_specs=[sm, vm, hbm, hbm, hbm, hbm, hbm, hbm],
+        in_specs=[sm, vm, vm, vm, hbm, hbm, hbm, hbm, hbm],
         out_specs=(vm, vm, vm),
         scratch_shapes=[
             pltpu.VMEM((NT, 4, 16, PW), BF16),
@@ -426,22 +440,23 @@
             pltpu.VMEM((16, 128), F32),
             pltpu.VMEM((16, 128), F32),
             pltpu.VMEM((64, 128), BF16),
-            dma((7,)),
+            dma((6,)),
             dma((4,)),
             dma((NY,)),
             dma((NY,)),
             dma((4, 4, NSPLIT)),
             dma((NZ,)),
             dma((NZ,)),
-            dma((11,)),
+            dma((13,)),
             dma((16,)),
         ],
         compiler_params=pltpu.CompilerParams(collective_id=0, has_side_effects=True),
         name="logra",
     )(
         plan.reshape(16),
-        valid,
-        pt,
+        validity,
+        proj_in.T,
+        proj_out.T,
         activations,
         out_grads,
         precond,

time: 145 us -> 86.9 us (0.60)
  Pallas kernels: 135 us -> 81.4 us
  other arithmetic: 3.62 us -> 0 us
    pallas_call x1, Pallas kernels: 135 us -> 81.4 us  [local(): pl.pallas_call(kernel, out_shape=(jax.ShapeDtypeStruct((1024, 128), F32),...]
where the time goes in v2:
time: 86.9 us; the launch traced here: 86.6 us
  Pallas kernels  81.4 us (94%)
  local copies, waits for them, and re-layouts  4.5 us (5%)
    pallas_call x1, Pallas kernels, local(): pl.pallas_call(kernel, out_shape=(jax.ShapeDtypeStruct((1024, 128), F32),...  81.4 us
    unnamed x2, local copies, waits for them, and re-layouts  3.06 us

profile of v2, /device:TPU:1, one launch (start us, length us, event | category | flops | bytes accessed | tf_op | source)
XLA Modules:
  0.0 86.6 jit_solution(3165421288535273046)
XLA Ops:
  0.6 81.4 %logra.1 = (f32[1024,128]{1,0:T(8,128)}, f32[2,128]{1,0:T(2,128)}, f32[64,32]{1,0:T(8,128)}) custom-call(s32[16]{0:T(128)} %bitcast.7, s32[2,32]{1,0:T(2,128)} %valid_ref.1, bf16[64,448]{1,0:T(8,128)(2,1)} %bitcast.5, bf16[64,128]{1,0:T(8,128)(2,1)} %bitcast.6, bf16[2,32,14336]{2,1,0:T(8,128)(2,1)} %act_ref.1, bf16[2,32,4096]{2,1,0:T(8,128)(2,1)} %og_ref.1, ...), custom_call_target="tpu_custom_call" | custom-call | tf_op jit(solution)/shard_map/logra/pallas_call | solution.py:416
  82.1 1.4 %copy.12 = f32[64,32]{0,1:T(8,128)} copy(f32[64,32]{1,0:T(8,128)} %get-tuple-element.5) | data formatting | bytes 16384 | tf_op jit(solution)/shard_map/logra/pallas_call | solution.py:416
  83.5 1.9 %copy.15 = f32[1024,128]{1,0:T(8,128)} copy(f32[1024,128]{1,0:T(8,128)} %get-tuple-element.9) | data formatting | bytes 1048576
  85.4 1.2 %copy.16 = f32[2,128]{1,0:T(2,128)} copy(f32[2,128]{1,0:T(2,128)} %get-tuple-element.10) | data formatting | bytes 2048

commit v3 on v2

--- a/solution.py
+++ b/solution.py
@@ -22,10 +22,11 @@
 NSPLIT = 2
 NZ = 8 * NSPLIT
 ZCOLS = QCOLS // NSPLIT
-LAG = 2
+LAG = 3
 PLAN_Y = 1
-PLAN_RS = 6
+PLAN_RS = 3
 PLAN_AG = 4
+PLAN_AR = 3
 
 
 def nt_dot(a, b):
@@ -35,7 +36,7 @@
 def kernel(
     plan_ref, valid_ref, pin_ref, pout_ref, act_ref, og_ref, prec_ref, q_ref, rows_ref,
     scores_ref, pdoc_ref, dsc_ref,
-    ptall, act, og, rows, rowsb, qall, rall, part, rsbuf, gown, gt, gs, ary, arz, arsrc, arsrc2, qp,
+    ptall, act, og, rows, rowsb, qall, rall, part, rsbuf, gown, gt, gs, ary, arz, arsrc, arsrc2,
     lsem, pz_r, pyu_r, pyd_r, xs_r, zu_r, zd_r, one_r, snd,
 ):
     t = lax.axis_index("tok")
@@ -95,16 +96,15 @@
     def greet(dev):
         pl.semaphore_signal(barrier, inc=1, device_id=dev, device_id_type=MESH)
 
-    greet(at_z(1))
-    greet(at_z(-1))
-
-    @pl.loop(1, NT)
-    def _(k):
-        greet(((t + k) % NT, s))
-
-    @pl.loop(1, NS)
-    def _(k):
-        greet((t, (s + k) % NS))
+    greet(partner)
+    greet((t, other))
+    for d in (1, -1, 2):
+        greet(at_x(d))
+    for d in (1, -1):
+        greet(at_y(d))
+        greet(at_z(d))
+    for d in (1, 2, 3):
+        greet((((zl + d) % 4) * 8 + y, s))
 
     win = pin_ref[...]
     gap = jnp.zeros((64, WIN - 448), BF16)
@@ -118,7 +118,7 @@
         ptall[t, :, :, :WIN] = jnp.concatenate([gap, win], axis=1).reshape(4, 16, WIN)
 
     ptall[t, :, :, WIN:] = pout_ref[...].reshape(4, 16, PW - WIN)
-    pl.semaphore_wait(barrier, NT - 1 + NS - 1 + 2)
+    pl.semaphore_wait(barrier, 12)
 
     half = pl.ds(2 * c, 2)
 
@@ -272,6 +272,7 @@
     pwait(pz_r.at[2], 1)
     pwait(pz_r.at[3], 1)
     ysend(3)
+    zrun(2)
     pshare(slot(0, 2))
     for k in range(4, NY):
         ysend(k)
@@ -296,9 +297,11 @@
         return left, right
 
     drain(ptall.at[pl.ds(0, 19), pl.ds(0, 2)], one_r.at[R_PSH])
+    zrun(1)
     acc = project((jnp.zeros((64, 64), F32), jnp.zeros((64, 64), F32)), (0, -1, 1, -2, 2))
     yrecv_to(0, NY)
     yrecv_to(1, NY)
+    zrun(1)
     drain(rall.at[pl.ds(0, 3)], one_r.at[R_RX])
     drain(ptall.at[pl.ds(0, 12), pl.ds(0, 2)], one_r.at[R_PSH2])
     left, right = project(acc, (-3, 3, 4))
@@ -315,6 +318,14 @@
         outer = jnp.dot(masked, left, preferred_element_type=F32)
         part[:, d, :] = jnp.concatenate([outer[:32], outer[32:]], axis=1)
 
+    l_pr.wait()
+    drain(rall.at[pl.ds(0, 3)], one_r.at[R_RX2])
+
+    @pl.loop(0, 8)
+    def _(k):
+        ref = rall.at[2 * k + c]
+        rcopy(ref, ref, snd.at[S_RSH], one_r.at[R_RSH], partner).start()
+
     @pl.loop(1, NT)
     def _(k):
         to = (t + k) % NT
@@ -322,8 +333,12 @@
 
     rsbuf[t] = part[t]
     zrun(PLAN_RS)
-    drain(qall.at[pl.ds(0, 4)], one_r.at[R_QSA])
-    score(zh)
+    drain(rall.at[pl.ds(0, 8)], one_r.at[R_RSH])
+    prows = rall[...].astype(F32).reshape(128, 4096).astype(BF16)
+    own_q = jnp.concatenate(
+        [jnp.concatenate([qall[s, k, j] for j in range(NSPLIT)], axis=1) for k in range(4)], axis=0
+    )
+    qp = nt_dot(own_q, prows).astype(BF16)
     drain(rsbuf.at[pl.ds(0, NT - 1)], one_r.at[R_RS])
     total = jnp.sum(rsbuf[...], axis=0) * (1.0 / 32.0)
     gown[...] = total.astype(BF16).astype(F32)
@@ -338,30 +353,17 @@
     def _(k):
         rcopy(gown, gt.at[t], snd.at[S_GT], one_r.at[R_GT], ((t + k) % NT, s)).start()
 
-    l_pr.wait()
-    drain(rall.at[pl.ds(0, 3)], one_r.at[R_RX2])
-
-    @pl.loop(0, 8)
-    def _(k):
-        ref = rall.at[2 * k + c]
-        rcopy(ref, ref, snd.at[S_RSH], one_r.at[R_RSH], partner).start()
-
     zrun(PLAN_AG)
-    drain(rall.at[pl.ds(0, 8)], one_r.at[R_RSH])
-    prows = rall[...].astype(F32).reshape(128, 4096).astype(BF16)
-    for k in range(4):
-        own_q = jnp.concatenate([qall[s, k, j] for j in range(NSPLIT)], axis=1)
-        qp[pl.ds(16 * k, 16), :] = nt_dot(own_q, prows).astype(BF16)
-
     drain(gs.at[pl.ds(0, NS - 1)], one_r.at[R_GS])
     docs = jnp.concatenate([gs[:, 0, :], gs[:, 1, :]], axis=0)
     acc = jnp.zeros((16, 128), F32)
-    d0 = lax.broadcasted_iota(jnp.int32, (128, 32), 0)
-    d1 = lax.broadcasted_iota(jnp.int32, (128, 32), 1)
-    for j in range(4):
-        put = (d0 == 32 * j + 2 * (d1 % 16) + d1 // 16).astype(F32).astype(BF16)
-        spread = jnp.dot(put, docs.astype(BF16), preferred_element_type=F32).astype(BF16)
-        acc = acc + nt_dot(qp[pl.ds(16 * j, 16), :], spread)
+    d0 = lax.broadcasted_iota(jnp.int32, (16, 32), 0)
+    d1 = lax.broadcasted_iota(jnp.int32, (16, 32), 1)
+    none = jnp.zeros((64, 128), BF16)
+    for h in range(2):
+        put = (d0 + 16 * h == 2 * (d1 % 16) + d1 // 16).astype(F32).astype(BF16)
+        block = jnp.dot(put, docs.astype(BF16), preferred_element_type=F32).astype(BF16)
+        acc = acc + nt_dot(block, jnp.concatenate([qp, none] if h == 0 else [none, qp], axis=0))
     arsrc[...] = acc
     ary[y] = acc
 
@@ -369,6 +371,7 @@
     def _(k):
         rcopy(arsrc, ary.at[y], snd.at[S_ARY], one_r.at[R_ARY], at_y(k)).start()
 
+    zrun(PLAN_AR)
     drain(gt.at[pl.ds(0, NT - 1)], one_r.at[R_GT])
     pdoc_ref[...] = nt_dot(jnp.concatenate([gt[i] for i in range(NT)], axis=1).astype(BF16), prows)
 
@@ -381,14 +384,15 @@
     def _(k):
         rcopy(arsrc2, arz.at[zl], snd.at[S_ARZ], one_r.at[R_ARZ], (((zl + k) % 4) * 8 + y, s)).start()
 
+    drain(qall.at[pl.ds(0, 4)], one_r.at[R_QSA])
+    score(zh)
     zrun(nsteps)
     drain(qall.at[pl.ds(0, 4)], one_r.at[R_QSB])
     score(1 - zh)
 
     drain(arz.at[pl.ds(0, 3)], one_r.at[R_ARZ])
     acc = jnp.sum(arz[...], axis=0)
-    for j in range(4):
-        dsc_ref[pl.ds(16 * j, 16), :] = acc[:, 32 * j : 32 * j + 32]
+    dsc_ref[...] = jnp.concatenate([acc[:, :64], acc[:, 64:]], axis=0)
 
     sent(ptall.at[pl.ds(0, 2), pl.ds(0, 2)], snd.at[S_PZ])
     sent(ptall.at[0, pl.ds(0, 2)], snd.at[S_PZH])
@@ -408,17 +412,23 @@
     sent(arz.at[pl.ds(0, 3)], snd.at[S_ARZ])
 
 
+def hand_over(a_ref, b_ref, c_ref, a_out, b_out, c_out):
+    a_out[...] = a_ref[...]
+    b_out[...] = b_ref[...]
+    c_out[...] = c_ref[...]
+
+
 def local(activations, out_grads, validity, proj_in, proj_out, precond, queries, store_rows, plan):
     hbm = pl.BlockSpec(memory_space=pl.ANY)
     vm = pl.BlockSpec(memory_space=pltpu.VMEM)
     sm = pl.BlockSpec(memory_space=pltpu.SMEM)
     dma = pltpu.SemaphoreType.DMA
-    return pl.pallas_call(
+    made = pl.pallas_call(
         kernel,
         out_shape=(
             jax.ShapeDtypeStruct((1024, 128), F32),
             jax.ShapeDtypeStruct((2, 128), F32),
-            jax.ShapeDtypeStruct((64, 32), F32),
+            jax.ShapeDtypeStruct((32, 64), F32),
         ),
         in_specs=[sm, vm, vm, vm, hbm, hbm, hbm, hbm, hbm],
         out_specs=(vm, vm, vm),
@@ -439,7 +449,6 @@
             pltpu.VMEM((4, 16, 128), F32),
             pltpu.VMEM((16, 128), F32),
             pltpu.VMEM((16, 128), F32),
-            pltpu.VMEM((64, 128), BF16),
             dma((6,)),
             dma((4,)),
             dma((NY,)),
@@ -463,6 +472,14 @@
         queries.reshape(4, 16, 4096),
         store_rows,
     )
+    scores, precond_docs, doc_scores = pl.pallas_call(
+        hand_over,
+        out_shape=tuple(jax.ShapeDtypeStruct(m.shape, m.dtype) for m in made),
+        in_specs=[vm] * 3,
+        out_specs=(vm,) * 3,
+        name="hand_over",
+    )(*made)
+    return scores, precond_docs, doc_scores.T
 
 
 def solution(mesh):

time: 86.9 us -> 73.7 us (0.85)
  Pallas kernels: 81.4 us -> 72.9 us
  local copies, waits for them, and re-layouts: 4.5 us -> 0 us
    pallas_call x1, Pallas kernels: 81.4 us -> 71 us  [local(): pl.pallas_call(kernel, out_shape=(jax.ShapeDtypeStruct((1024, 128), F32),...]
    unnamed x2 -> x0, local copies, waits for them, and re-layouts: 3.06 us -> none
    pallas_call x0 -> x1, Pallas kernels: none -> 1.88 us  [local(): pl.pallas_call(hand_over, out_shape=tuple((jax.ShapeDtypeStruct(m.shape,...]
    pallas_call x1 -> x0, local copies, waits for them, and re-layouts: 1.44 us -> none  [local(): pl.pallas_call(kernel, out_shape=(jax.ShapeDtypeStruct((1024, 128), F32),...]
where the time goes in v3:
time: 73.7 us; the launch traced here: 73.5 us
  Pallas kernels  72.9 us (99%)
    pallas_call x1, Pallas kernels, local(): pl.pallas_call(kernel, out_shape=(jax.ShapeDtypeStruct((1024, 128), F32),...  71 us
    pallas_call x1, Pallas kernels, local(): pl.pallas_call(hand_over, out_shape=tuple((jax.ShapeDtypeStruct(m.shape,...  1.88 us

profile of v3, /device:TPU:1, one launch (start us, length us, event | category | flops | bytes accessed | tf_op | source)
XLA Modules:
  0.0 73.5 jit_solution(4420901769463479701)
XLA Ops:
  0.6 71.0 %logra.1 = (f32[1024,128]{1,0:T(8,128)}, f32[2,128]{1,0:T(2,128)}, f32[32,64]{1,0:T(8,128)}) custom-call(s32[16]{0:T(128)} %bitcast.8, s32[2,32]{1,0:T(2,128)} %valid_ref.1, bf16[64,448]{1,0:T(8,128)(2,1)} %bitcast.6, bf16[64,128]{1,0:T(8,128)(2,1)} %bitcast.7, bf16[2,32,14336]{2,1,0:T(8,128)(2,1)} %act_ref.1, bf16[2,32,4096]{2,1,0:T(8,128)(2,1)} %og_ref.1, ...), custom_call_target="tpu_custom_call" | custom-call | tf_op jit(solution)/shard_map/logra/pallas_call | solution.py:426
  71.7 1.9 %hand_over.1 = (f32[1024,128]{1,0:T(8,128)}, f32[2,128]{1,0:T(2,128)}, f32[32,64]{1,0:T(8,128)}) custom-call(f32[1024,128]{1,0:T(8,128)} %get-tuple-element.9.a_ref, f32[2,128]{1,0:T(2,128)} %get-tuple-element.10.b_ref, f32[32,64]{1,0:T(8,128)} %get-tuple-element.11.c_ref), custom_call_target="tpu_custom_call" | custom-call | tf_op jit(solution)/shard_map/hand_over/pallas_call | solution.py:475

commit v4 on v3

--- a/solution.py
+++ b/solution.py
@@ -19,6 +19,7 @@
 UP = [(0, 0), (0, -1), (0, 1), (0, 2)] + [(-k, d) for k in (1, 2) for d in (0, -1, 1, 2)] + [(-3, 0), (-3, -1)]
 DN = [(0, 0), (0, 1), (0, -1), (0, 2)] + [(k, d) for k in (1, 2) for d in (0, 1, -1, 2)] + [(3, 1), (3, 2)]
 NY = len(UP)
+DYS = (0, -1, 1, -2, 2, -3, 3, 4)
 NSPLIT = 2
 NZ = 8 * NSPLIT
 ZCOLS = QCOLS // NSPLIT
@@ -37,7 +38,7 @@
     plan_ref, valid_ref, pin_ref, pout_ref, act_ref, og_ref, prec_ref, q_ref, rows_ref,
     scores_ref, pdoc_ref, dsc_ref,
     ptall, act, og, rows, rowsb, qall, rall, part, rsbuf, gown, gt, gs, ary, arz, arsrc, arsrc2,
-    lsem, pz_r, pyu_r, pyd_r, xs_r, zu_r, zd_r, one_r, snd,
+    lsem, pz_r, pb_r, pyu_r, pyd_r, xs_r, zu_r, zd_r, one_r, snd,
 ):
     t = lax.axis_index("tok")
     s = lax.axis_index("store")
@@ -73,7 +74,7 @@
         return q_ref.at[k, :, pl.ds(j * ZCOLS, ZCOLS)]
 
     R_PSH, R_PSH2, R_QSA, R_QSB, R_RZ, R_RX, R_RX2, R_RSH, R_RS, R_GT, R_GS, R_ARY, R_ARZ = range(13)
-    (S_PZ, S_PZH, S_PY, S_PSH, S_X, S_Z, S_QSH, S_RZ, S_RX, S_RX2, S_RSH, S_RS, S_GT, S_GS, S_ARY, S_ARZ) = range(16)
+    (S_PZ, S_PZH, S_PY, S_PSH, S_X, S_Z, S_QSH, S_RZ, S_RX, S_RX2, S_RSH, S_RS, S_GT, S_GS, S_ARY, S_ARZ, S_PB) = range(17)
 
     loc = []
 
@@ -120,7 +121,7 @@
     ptall[t, :, :, WIN:] = pout_ref[...].reshape(4, 16, PW - WIN)
     pl.semaphore_wait(barrier, 12)
 
-    half = pl.ds(2 * c, 2)
+    qa, qb = pl.ds(2 * c, 1), pl.ds(2 * c + 1, 1)
 
     def slot(dy, dz):
         return ((zl + 4 + dz) % 4) * 8 + (y + 8 + dy) % 8
@@ -129,14 +130,79 @@
         ref = ptall.at[sl, rowsl]
         rcopy(ref, ref, ss, rs, dev).start()
 
-    def pshare(sl, group=None):
-        psend(sl, half, snd.at[S_PSH], one_r.at[R_PSH if group is None else group], partner)
-
-    psend(t, half, snd.at[S_PZ], pz_r.at[0], at_z(1))
-    psend(t, half, snd.at[S_PZ], pz_r.at[1], at_z(-1))
-
-    def pwait(sem, n=2):
-        drain(ptall.at[0, pl.ds(0, n)], sem)
+    def pshare(dy, dz, q):
+        psend(slot(dy, dz), q, snd.at[S_PSH], one_r.at[R_PSH if abs(dy) <= 2 else R_PSH2], partner)
+
+    def pwait(sem):
+        drain(ptall.at[0, pl.ds(0, 1)], sem)
+
+    def bsend(dy, dz, n, dev):
+        psend(slot(dy, dz), qb, snd.at[S_PB], pb_r.at[n], dev)
+
+    def bz_send(i):
+        bsend(DYS[i], 0, 7 + i, at_z(1))
+        bsend(DYS[i], 0, 15 + i, at_z(-1))
+
+    def bz_recv(i):
+        pwait(pb_r.at[7 + i])
+        if i % 2 == 0:
+            bsend(DYS[i], -1, 23 + i, at_z(1))
+        pwait(pb_r.at[15 + i])
+        if i % 2 == 1:
+            bsend(DYS[i], 1, 23 + i, at_z(-1))
+        pshare(DYS[i], -1, qb)
+        pshare(DYS[i], 1, qb)
+
+    def bz_fin(i):
+        pwait(pb_r.at[23 + i])
+        pshare(DYS[i], 2, qb)
+
+    def by_recv(r):
+        pwait(pb_r.at[r - 1])
+        if r <= 3:
+            bsend(-r, 0, r, at_y(1))
+            pwait(pb_r.at[3 + r])
+            if r <= 2:
+                bsend(r, 0, 4 + r, at_y(-1))
+        for i in {1: (1, 2), 2: (3, 4), 3: (5, 6), 4: (7,)}[r]:
+            bz_send(i)
+            pshare(DYS[i], 0, qb)
+
+    got = set()
+
+    def yrecv(side, k):
+        if (side, k) in got:
+            return
+        got.add((side, k))
+        order, sems, d = ((UP, pyu_r, -1), (DN, pyd_r, 1))[side]
+        pwait(sems.at[k])
+        pshare(order[k][0] + d, order[k][1], qa)
+
+    def usend(*ks):
+        for k in ks:
+            dy, dz = UP[k]
+            if dy:
+                yrecv(0, UP.index((dy + 1, dz)))
+            psend(slot(dy, dz), qa, snd.at[S_PY], pyu_r.at[k], at_y(1))
+
+    def dsend(*ks):
+        for k in ks:
+            dy, dz = DN[k]
+            if dy:
+                yrecv(1, DN.index((dy - 1, dz)))
+            psend(slot(dy, dz), qa, snd.at[S_PY], pyd_r.at[k], at_y(-1))
+
+    def both(*ks):
+        for k in ks:
+            usend(k)
+            dsend(k)
+
+    psend(t, qa, snd.at[S_PZ], pz_r.at[0], at_z(1))
+    psend(t, qa, snd.at[S_PZ], pz_r.at[1], at_z(-1))
+    bsend(0, 0, 0, at_y(1))
+    bsend(0, 0, 4, at_y(-1))
+    both(0)
+    bz_send(0)
 
     for k in (0, 2, 1, 3):
         for j in range(NSPLIT):
@@ -147,26 +213,6 @@
     rcopy(prec_ref, rall.at[s], snd.at[S_RZ], one_r.at[R_RZ], (t, other)).start()
     for d in (1, -1, 2):
         rcopy(prec_ref, rall.at[s], snd.at[S_RX], one_r.at[R_RX], at_x(d)).start()
-
-    def need(order, k, d):
-        dy, dz = order[k]
-        return 0 if dy == 0 else order.index((dy + d, dz)) + 1
-
-    got = [0, 0]
-
-    def yrecv_to(side, n):
-        order, sems, d = ((UP, pyu_r, -1), (DN, pyd_r, 1))[side]
-        while got[side] < n:
-            k = got[side]
-            pwait(sems.at[k])
-            pshare(slot(order[k][0] + d, order[k][1]), R_PSH if k < 8 else R_PSH2)
-            got[side] += 1
-
-    def ysend(k):
-        yrecv_to(0, need(UP, k, 1))
-        psend(slot(*UP[k]), half, snd.at[S_PY], pyu_r.at[k], at_y(1))
-        yrecv_to(1, need(DN, k, -1))
-        psend(slot(*DN[k]), half, snd.at[S_PY], pyd_r.at[k], at_y(-1))
 
     def xorder(i):
         return i + i // 2 - 2 * (i // 3)
@@ -260,23 +306,47 @@
                 w = plan_ref[sl + h].astype(F32)
                 scores_ref[pl.ds(pl.multiple_of(64 * (sl + h), 64), 64), :] = raw[64 * h : 64 * h + 64] * w
 
-    ysend(0)
     pwait(pz_r.at[0])
-    psend(slot(0, -1), pl.ds(2 * c, 1), snd.at[S_PZH], pz_r.at[2], at_z(1))
+    psend(slot(0, -1), qa, snd.at[S_PZH], pz_r.at[2], at_z(1))
     pwait(pz_r.at[1])
-    psend(slot(0, 1), pl.ds(2 * c + 1, 1), snd.at[S_PZH], pz_r.at[3], at_z(-1))
-    ysend(1)
-    ysend(2)
-    pshare(slot(0, -1))
-    pshare(slot(0, 1))
-    pwait(pz_r.at[2], 1)
-    pwait(pz_r.at[3], 1)
-    ysend(3)
+    both(1, 2)
+    by_recv(1)
+    both(4)
+    pshare(0, -1, qa)
+    pshare(0, 1, qa)
+    bz_recv(0)
     zrun(2)
-    pshare(slot(0, 2))
-    for k in range(4, NY):
-        ysend(k)
-        zrun(PLAN_Y)
+    pwait(pz_r.at[2])
+    both(3)
+    by_recv(2)
+    both(5, 6, 8)
+    pshare(0, 2, qa)
+    for i in (1, 2):
+        bz_recv(i)
+    bz_fin(0)
+    zrun(3)
+    by_recv(3)
+    both(7, 9, 10)
+    usend(12)
+    for i in (3, 4):
+        bz_recv(i)
+    for i in (1, 2):
+        bz_fin(i)
+    zrun(3)
+    by_recv(4)
+    both(11)
+    usend(13)
+    dsend(12)
+    for i in (5, 6):
+        bz_recv(i)
+    for i in (3, 4):
+        bz_fin(i)
+    zrun(3)
+    dsend(13)
+    bz_recv(7)
+    for k in range(8):
+        yrecv(0, k)
+        yrecv(1, k)
     drain(rall.at[0], one_r.at[R_RZ])
     for d in (1, -1, 2):
         rcopy(rall.at[other], rall.at[other], snd.at[S_RX2], one_r.at[R_RX2], at_x(d)).start()
@@ -297,10 +367,13 @@
         return left, right
 
     drain(ptall.at[pl.ds(0, 19), pl.ds(0, 2)], one_r.at[R_PSH])
-    zrun(1)
+    zrun(2)
     acc = project((jnp.zeros((64, 64), F32), jnp.zeros((64, 64), F32)), (0, -1, 1, -2, 2))
-    yrecv_to(0, NY)
-    yrecv_to(1, NY)
+    for i in (5, 6, 7):
+        bz_fin(i)
+    for k in range(NY):
+        yrecv(0, k)
+        yrecv(1, k)
     zrun(1)
     drain(rall.at[pl.ds(0, 3)], one_r.at[R_RX])
     drain(ptall.at[pl.ds(0, 12), pl.ds(0, 2)], one_r.at[R_PSH2])
@@ -394,9 +467,10 @@
     acc = jnp.sum(arz[...], axis=0)
     dsc_ref[...] = jnp.concatenate([acc[:, :64], acc[:, 64:]], axis=0)
 
-    sent(ptall.at[pl.ds(0, 2), pl.ds(0, 2)], snd.at[S_PZ])
-    sent(ptall.at[0, pl.ds(0, 2)], snd.at[S_PZH])
-    sent(ptall.at[pl.ds(0, 2 * NY), pl.ds(0, 2)], snd.at[S_PY])
+    sent(ptall.at[0, pl.ds(0, 2)], snd.at[S_PZ])
+    sent(ptall.at[0, pl.ds(0, 1)], snd.at[S_PZH])
+    sent(ptall.at[pl.ds(0, NY), pl.ds(0, 2)], snd.at[S_PY])
+    sent(ptall.at[pl.ds(0, 31), pl.ds(0, 1)], snd.at[S_PB])
     sent(ptall.at[pl.ds(0, NT - 1), pl.ds(0, 2)], snd.at[S_PSH])
     sent(qall.at[pl.ds(0, 3)], snd.at[S_X])
     sent(qall.at[pl.ds(0, 4)], snd.at[S_Z])
@@ -450,14 +524,15 @@
             pltpu.VMEM((16, 128), F32),
             pltpu.VMEM((16, 128), F32),
             dma((6,)),
-            dma((4,)),
+            dma((3,)),
+            dma((31,)),
             dma((NY,)),
             dma((NY,)),
             dma((4, 4, NSPLIT)),
             dma((NZ,)),
             dma((NZ,)),
             dma((13,)),
-            dma((16,)),
+            dma((17,)),
         ],
         compiler_params=pltpu.CompilerParams(collective_id=0, has_side_effects=True),
         name="logra",

time: 73.7 us -> 74.1 us (level)
  no operation moved by 1% of the time
where the time goes in v4:
time: 74.1 us; the launch traced here: 73.9 us
  Pallas kernels  73.3 us (99%)
    pallas_call x1, Pallas kernels, local(): pl.pallas_call(kernel, out_shape=(jax.ShapeDtypeStruct((1024, 128), F32),...  71.4 us
    pallas_call x1, Pallas kernels, local(): pl.pallas_call(hand_over, out_shape=tuple((jax.ShapeDtypeStruct(m.shape,...  1.88 us

profile of v4, /device:TPU:1, one launch (start us, length us, event | category | flops | bytes accessed | tf_op | source)
XLA Modules:
  0.0 73.9 jit_solution(13506797089168365771)
XLA Ops:
  0.6 71.4 %logra.1 = (f32[1024,128]{1,0:T(8,128)}, f32[2,128]{1,0:T(2,128)}, f32[32,64]{1,0:T(8,128)}) custom-call(s32[16]{0:T(128)} %bitcast.8, s32[2,32]{1,0:T(2,128)} %valid_ref.1, bf16[64,448]{1,0:T(8,128)(2,1)} %bitcast.6, bf16[64,128]{1,0:T(8,128)(2,1)} %bitcast.7, bf16[2,32,14336]{2,1,0:T(8,128)(2,1)} %act_ref.1, bf16[2,32,4096]{2,1,0:T(8,128)(2,1)} %og_ref.1, ...), custom_call_target="tpu_custom_call" | custom-call | tf_op jit(solution)/shard_map/logra/pallas_call | solution.py:500
  72.0 1.9 %hand_over.1 = (f32[1024,128]{1,0:T(8,128)}, f32[2,128]{1,0:T(2,128)}, f32[32,64]{1,0:T(8,128)}) custom-call(f32[1024,128]{1,0:T(8,128)} %get-tuple-element.9.a_ref, f32[2,128]{1,0:T(2,128)} %get-tuple-element.10.b_ref, f32[32,64]{1,0:T(8,128)} %get-tuple-element.11.c_ref), custom_call_target="tpu_custom_call" | custom-call | tf_op jit(solution)/shard_map/hand_over/pallas_call | solution.py:550

commit v5 on v3

--- a/solution.py
+++ b/solution.py
@@ -20,7 +20,7 @@
 DN = [(0, 0), (0, 1), (0, -1), (0, 2)] + [(k, d) for k in (1, 2) for d in (0, 1, -1, 2)] + [(3, 1), (3, 2)]
 NY = len(UP)
 NSPLIT = 2
-NZ = 8 * NSPLIT
+NZ = 6 * NSPLIT
 ZCOLS = QCOLS // NSPLIT
 LAG = 3
 PLAN_Y = 1
@@ -37,7 +37,7 @@
     plan_ref, valid_ref, pin_ref, pout_ref, act_ref, og_ref, prec_ref, q_ref, rows_ref,
     scores_ref, pdoc_ref, dsc_ref,
     ptall, act, og, rows, rowsb, qall, rall, part, rsbuf, gown, gt, gs, ary, arz, arsrc, arsrc2,
-    lsem, pz_r, pyu_r, pyd_r, xs_r, zu_r, zd_r, one_r, snd,
+    lsem, pz_r, pyu_r, pyd_r, xs_r, zu_r, zd_r, xo_r, one_r, snd,
 ):
     t = lax.axis_index("tok")
     s = lax.axis_index("store")
@@ -189,7 +189,7 @@
         return qall.at[zh * 8 + ((x + [0, 1, 3, 2][xi]) % 4) * 2 + c, k, j]
 
     def zstep(tau):
-        if tau < NZ:
+        if tau < 8 * NSPLIT:
             xi, k, j = tau // (2 * NSPLIT), (tau // NSPLIT) % 2, tau % NSPLIT
             for i in {0: (0,), 1: (1, 2), 2: (), 3: (3,)}[xi]:
                 for kk in (k, k + 2):
@@ -225,6 +225,10 @@
 
             qshare(ref, R_QSB)
 
+            @pl.when((u >= 2 * NSPLIT) & (u < 4 * NSPLIT))
+            def _():
+                rcopy(ref, ref, snd.at[S_X], xo_r.at[u - 2 * NSPLIT], at_x(-1)).start()
+
         v = tau - LAG * (4 - zl)
 
         @pl.when((v >= 0) & (v < NZ))
@@ -237,6 +241,10 @@
                 rcopy(ref, ref, snd.at[S_Z], zd_r.at[v], at_z(-1)).start()
 
             qshare(ref, R_QSB)
+
+            @pl.when(v >= 4 * NSPLIT)
+            def _():
+                rcopy(ref, ref, snd.at[S_X], xo_r.at[v - 2 * NSPLIT], at_x(1)).start()
 
     nsteps = NZ + 4 * LAG
     zs = iter(range(nsteps))
@@ -387,6 +395,10 @@
     drain(qall.at[pl.ds(0, 4)], one_r.at[R_QSA])
     score(zh)
     zrun(nsteps)
+    for n in range(4 * NSPLIT):
+        ref = qall.at[(1 - zh) * 8 + ((x + 2) % 4) * 2 + c, n // NSPLIT, n % NSPLIT]
+        drain(ref, xo_r.at[n])
+        qshare(ref, R_QSB)
     drain(qall.at[pl.ds(0, 4)], one_r.at[R_QSB])
     score(1 - zh)
 
@@ -398,8 +410,8 @@
     sent(ptall.at[0, pl.ds(0, 2)], snd.at[S_PZH])
     sent(ptall.at[pl.ds(0, 2 * NY), pl.ds(0, 2)], snd.at[S_PY])
     sent(ptall.at[pl.ds(0, NT - 1), pl.ds(0, 2)], snd.at[S_PSH])
-    sent(qall.at[pl.ds(0, 3)], snd.at[S_X])
-    sent(qall.at[pl.ds(0, 4)], snd.at[S_Z])
+    sent(qall.at[pl.ds(0, 4)], snd.at[S_X])
+    sent(qall.at[pl.ds(0, 3)], snd.at[S_Z])
     sent(qall.at[pl.ds(0, 8)], snd.at[S_QSH])
     sent(rall.at[0], snd.at[S_RZ])
     sent(rall.at[pl.ds(0, 3)], snd.at[S_RX])
@@ -456,6 +468,7 @@
             dma((4, 4, NSPLIT)),
             dma((NZ,)),
             dma((NZ,)),
+            dma((4 * NSPLIT,)),
             dma((13,)),
             dma((16,)),
         ],

time: 73.7 us -> 72.4 us (0.982)
  Pallas kernels: 72.9 us -> 71.5 us
    pallas_call x1, Pallas kernels: 71 us -> 69.7 us  [local(): pl.pallas_call(kernel, out_shape=(jax.ShapeDtypeStruct((1024, 128), F32),...]
where the time goes in v5:
time: 72.4 us; the launch traced here: 72.2 us
  Pallas kernels  71.5 us (99%)
    pallas_call x1, Pallas kernels, local(): pl.pallas_call(kernel, out_shape=(jax.ShapeDtypeStruct((1024, 128), F32),...  69.7 us
    pallas_call x1, Pallas kernels, local(): pl.pallas_call(hand_over, out_shape=tuple((jax.ShapeDtypeStruct(m.shape,...  1.88 us

profile of v5, /device:TPU:1, one launch (start us, length us, event | category | flops | bytes accessed | tf_op | source)
XLA Modules:
  0.0 72.2 jit_solution(5884698668553004020)
XLA Ops:
  0.6 69.7 %logra.1 = (f32[1024,128]{1,0:T(8,128)}, f32[2,128]{1,0:T(2,128)}, f32[32,64]{1,0:T(8,128)}) custom-call(s32[16]{0:T(128)} %bitcast.8, s32[2,32]{1,0:T(2,128)} %valid_ref.1, bf16[64,448]{1,0:T(8,128)(2,1)} %bitcast.6, bf16[64,128]{1,0:T(8,128)(2,1)} %bitcast.7, bf16[2,32,14336]{2,1,0:T(8,128)(2,1)} %act_ref.1, bf16[2,32,4096]{2,1,0:T(8,128)(2,1)} %og_ref.1, ...), custom_call_target="tpu_custom_call" | custom-call | tf_op jit(solution)/shard_map/logra/pallas_call | solution.py:438
  70.3 1.9 %hand_over.1 = (f32[1024,128]{1,0:T(8,128)}, f32[2,128]{1,0:T(2,128)}, f32[32,64]{1,0:T(8,128)}) custom-call(f32[1024,128]{1,0:T(8,128)} %get-tuple-element.9.a_ref, f32[2,128]{1,0:T(2,128)} %get-tuple-element.10.b_ref, f32[32,64]{1,0:T(8,128)} %get-tuple-element.11.c_ref), custom_call_target="tpu_custom_call" | custom-call | tf_op jit(solution)/shard_map/hand_over/pallas_call | solution.py:488
